TPU v7x, 32 devices: a whole 2x2x4 slice. The times are simulated.
32 devices in a mesh: dp: 32 (over z, y, x, core).
Axes of the slice: x: 2, y: 2, z: 4, core: 2. Of those that a mesh axis runs over, the one named last changes fastest.
Arguments:
- block_in: bfloat16 [12608, 768], P('dp'), may hold values from -6 to 6
- slot_mask: int32 [12608], P('dp'), may hold values from 0 to 1, as said below
- gain_first: bfloat16 [768], P('dp'), may hold values from 0.5 to 1.5
- shift_first: bfloat16 [768], P('dp'), may hold values from -3 to 3
- packed_weight: bfloat16 [768, 2304], P('dp'), may hold values from -0.21875 to 0.21875
- query_bias: bfloat16 [768], P('dp'), may hold values from -3 to 3
- value_bias: bfloat16 [768], P('dp'), may hold values from -3 to 3
- out_weight: bfloat16 [768, 768], P('dp'), may hold values from -1.75 to 1.75
- out_bias: bfloat16 [768], P('dp'), may hold values from -3 to 3
- gain_second: bfloat16 [768], P('dp'), may hold values from 0.5 to 1.5
- shift_second: bfloat16 [768], P('dp'), may hold values from -3 to 3
- up_weight: bfloat16 [768, 3072], P('dp'), may hold values from -0.21875 to 0.21875
- up_bias: bfloat16 [3072], P('dp'), may hold values from -3 to 3
- down_weight: bfloat16 [3072, 768], P('dp'), may hold values from -0.109375 to 0.109375
- down_bias: bfloat16 [768], P('dp'), may hold values from -3 to 3
- cotangent: bfloat16 [12608, 768], P('dp'), may hold values from -6 to 6
Outputs:
- block_out: bfloat16 [12608, 768], P('dp')
- input_grad: float32 [12608, 768], P('dp')
- grad_gain_first: float32 [768], P('dp')
- grad_shift_first: float32 [768], P('dp')
- grad_packed_weight: float32 [768, 2304], P('dp')
- grad_query_bias: float32 [768], P('dp')
- grad_value_bias: float32 [768], P('dp')
- grad_out_weight: float32 [768, 768], P('dp')
- grad_out_bias: float32 [768], P('dp')
- grad_gain_second: float32 [768], P('dp')
- grad_shift_second: float32 [768], P('dp')
- grad_up_weight: float32 [768, 3072], P('dp')
- grad_up_bias: float32 [3072], P('dp')
- grad_down_weight: float32 [3072, 768], P('dp')
- grad_down_bias: float32 [768], P('dp')
Inputs may be any that keep to these rules, and one draw needn't show every extreme that they name: `slot_mask`: each image slot of 197 tokens is all ones or all zeros; on each device the live image slots come first; each device has at least 1 of its 2 image slots live, and some device has both live.
All inputs are finite; a program needn't handle non-finite values.
Results may differ from a plain program's by a relative error of at most 0.011.
Values may be sent and summed in bfloat16 or wider, within the bound.
No kernel may reach another device: no remote copies, remote signals or barrier semaphores. Data moves between devices by JAX's collectives and lax.ppermute only.
A program may use at most 192 MiB of HBM per device.

v0:
```python
import jax
import jax.numpy as jnp
from jax import lax
from jax.sharding import PartitionSpec as P

D = 768
HEADS = 12
HEAD_DIM = 64
LEN = 197


def layer_norm(values, gain, shift):
    centre_mean = jnp.mean(values, axis=-1, keepdims=True)
    centred = values - centre_mean
    variance = jnp.mean(centred * centred, axis=-1, keepdims=True)
    return centred * lax.rsqrt(variance + 1e-06) * gain + shift


def token_sum(values):
    return jnp.sum(values, axis=(0, 1), dtype=jnp.float32)


def shards(
    block_in,
    slot_mask,
    gain_first,
    shift_first,
    packed_weight,
    query_bias,
    value_bias,
    out_weight,
    out_bias,
    gain_second,
    shift_second,
    up_weight,
    up_bias,
    down_weight,
    down_bias,
    cotangent,
):
    f32 = jnp.float32
    bf16 = jnp.bfloat16
    scale = HEAD_DIM ** (-0.5)
    attn_full = (
        lax.all_gather(gain_first, "dp", axis=0, tiled=True),
        lax.all_gather(shift_first, "dp", axis=0, tiled=True),
        lax.all_gather(packed_weight, "dp", axis=0, tiled=True),
        lax.all_gather(query_bias, "dp", axis=0, tiled=True),
        lax.all_gather(value_bias, "dp", axis=0, tiled=True),
        lax.all_gather(out_weight, "dp", axis=0, tiled=True),
        lax.all_gather(out_bias, "dp", axis=0, tiled=True),
    )
    mlp_full = (
        lax.all_gather(gain_second, "dp", axis=0, tiled=True),
        lax.all_gather(shift_second, "dp", axis=0, tiled=True),
        lax.all_gather(up_weight, "dp", axis=0, tiled=True),
        lax.all_gather(up_bias, "dp", axis=0, tiled=True),
        lax.all_gather(down_weight, "dp", axis=0, tiled=True),
        lax.all_gather(down_bias, "dp", axis=0, tiled=True),
    )
    full_g1, full_c1, full_packed, full_qbias, full_vbias, full_out, full_obias = attn_full
    full_g2, full_c2, full_up, full_ubias, full_down, full_dbias = mlp_full
    images = block_in.shape[0] // LEN
    inputs = block_in.astype(f32).reshape(images, LEN, D)
    live = slot_mask.astype(f32).reshape(images, LEN, 1)
    normed_low = layer_norm(inputs, full_g1.astype(f32), full_c1.astype(f32)).astype(bf16)
    packed = jnp.einsum("gtd,de->gte", normed_low, full_packed, preferred_element_type=f32)
    packed = packed.reshape(images, LEN, 3, HEADS, HEAD_DIM)
    query = (packed[:, :, 0] + full_qbias.astype(f32).reshape(HEADS, HEAD_DIM)).astype(bf16)
    key_low = packed[:, :, 1].astype(bf16)
    value_low = (packed[:, :, 2] + full_vbias.astype(f32).reshape(HEADS, HEAD_DIM)).astype(bf16)
    scores = jnp.einsum("gqhe,gkhe->ghqk", query, key_low, preferred_element_type=f32) * scale
    top_score = jnp.max(scores, axis=-1, keepdims=True)
    log_total = top_score + jnp.log(jnp.sum(jnp.exp(scores - top_score), axis=-1, keepdims=True))
    attn_low = jnp.exp(scores - log_total).astype(bf16)
    mixed = jnp.einsum("ghqk,gkhe->gqhe", attn_low, value_low, preferred_element_type=f32)
    attended = mixed.astype(bf16).reshape(images, LEN, D)
    branch = jnp.einsum(
        "gtd,de->gte", attended, full_out, preferred_element_type=f32
    ) + full_obias.astype(f32)
    middle = inputs + branch
    normed_two = layer_norm(middle, full_g2.astype(f32), full_c2.astype(f32)).astype(bf16)
    pre_act = jnp.einsum(
        "gtd,df->gtf", normed_two, full_up, preferred_element_type=f32
    ) + full_ubias.astype(f32)
    gelu_exact = lambda values: jax.nn.gelu(values, approximate=False)
    activated_f, gelu_pull = jax.vjp(gelu_exact, pre_act)
    activated = activated_f.astype(bf16)
    mlp_out = jnp.einsum(
        "gtf,fd->gtd", activated, full_down, preferred_element_type=f32
    ) + full_dbias.astype(f32)
    block_out = ((middle + mlp_out) * live).astype(bf16).reshape(images * LEN, D)
    back_g2, back_up, back_down = (
        lax.all_gather(gain_second, "dp", axis=0, tiled=True),
        lax.all_gather(up_weight, "dp", axis=0, tiled=True),
        lax.all_gather(down_weight, "dp", axis=0, tiled=True),
    )
    d_res = cotangent.astype(f32).reshape(images, LEN, D) * live
    d_mlp = d_res.astype(bf16)
    grad_down_bias = token_sum(d_mlp)
    grad_down_weight = jnp.einsum("gtf,gtd->fd", activated, d_mlp, preferred_element_type=f32)
    d_act = jnp.einsum("gtd,fd->gtf", d_mlp, back_down, preferred_element_type=f32)
    d_pre = gelu_pull(d_act)[0].astype(bf16)
    grad_up_bias = token_sum(d_pre)
    grad_up_weight = jnp.einsum("gtd,gtf->df", normed_two, d_pre, preferred_element_type=f32)
    d_normed_two = jnp.einsum("gtf,df->gtd", d_pre, back_up, preferred_element_type=f32)
    zero_shift = jnp.zeros((D,), f32)
    norm_pull_two = jax.vjp(layer_norm, middle, back_g2.astype(f32), zero_shift)[1]
    d_mid_part, grad_gain_second, grad_shift_second = norm_pull_two(d_normed_two)
    d_middle = d_res + d_mid_part
    mlp_grads = (
        grad_gain_second,
        grad_shift_second,
        grad_up_weight,
        grad_up_bias,
        grad_down_weight,
        grad_down_bias,
    )
    back_g1, back_packed, back_out = (
        lax.all_gather(gain_first, "dp", axis=0, tiled=True),
        lax.all_gather(packed_weight, "dp", axis=0, tiled=True),
        lax.all_gather(out_weight, "dp", axis=0, tiled=True),
    )
    d_branch = d_middle.astype(bf16)
    grad_out_bias = token_sum(d_branch)
    grad_out_weight = jnp.einsum("gtd,gte->de", attended, d_branch, preferred_element_type=f32)
    d_att = jnp.einsum("gte,de->gtd", d_branch, back_out, preferred_element_type=f32)
    d_att = d_att.astype(bf16).reshape(images, LEN, HEADS, HEAD_DIM)
    again = jnp.einsum("gqhe,gkhe->ghqk", query, key_low, preferred_element_type=f32) * scale
    attn_again = jnp.exp(again - log_total)
    d_values = jnp.einsum("ghqk,gqhe->gkhe", attn_low, d_att, preferred_element_type=f32).astype(
        bf16
    )
    d_attn = jnp.einsum("gqhe,gkhe->ghqk", d_att, value_low, preferred_element_type=f32)
    d_scores = (
        attn_again * (d_attn - jnp.sum(attn_again * d_attn, axis=-1, keepdims=True))
    ).astype(bf16)
    d_query = (
        jnp.einsum("ghqk,gkhe->gqhe", d_scores, key_low, preferred_element_type=f32) * scale
    ).astype(bf16)
    d_keys = (
        jnp.einsum("ghqk,gqhe->gkhe", d_scores, query, preferred_element_type=f32) * scale
    ).astype(bf16)
    grad_query_bias = token_sum(d_query).reshape(D)
    grad_value_bias = token_sum(d_values).reshape(D)
    d_packed = jnp.stack([d_query, d_keys, d_values], axis=2).reshape(images, LEN, 3 * D)
    grad_packed_weight = jnp.einsum("gtd,gte->de", normed_low, d_packed, preferred_element_type=f32)
    d_normed = jnp.einsum("gte,de->gtd", d_packed, back_packed, preferred_element_type=f32)
    norm_pull_one = jax.vjp(layer_norm, inputs, back_g1.astype(f32), zero_shift)[1]
    d_in_part, grad_gain_first, grad_shift_first = norm_pull_one(d_normed)
    input_grad = (d_middle + d_in_part).reshape(images * LEN, D)
    attn_grads = (
        grad_gain_first,
        grad_shift_first,
        grad_packed_weight,
        grad_query_bias,
        grad_value_bias,
        grad_out_weight,
        grad_out_bias,
    )
    owned_all = lax.psum_scatter(attn_grads + mlp_grads, "dp", scatter_dimension=0, tiled=True)
    owned_attn = owned_all[:7]
    owned_mlp = owned_all[7:]
    return (block_out, input_grad) + tuple(owned_attn) + tuple(owned_mlp)


def solution(mesh):
    in_specs = (
        P("dp", None),
        P("dp"),
        P("dp"),
        P("dp"),
        P("dp", None),
        P("dp"),
        P("dp"),
        P("dp", None),
        P("dp"),
        P("dp"),
        P("dp"),
        P("dp", None),
        P("dp"),
        P("dp", None),
        P("dp"),
        P("dp", None),
    )
    out_specs = (
        P("dp", None),
        P("dp", None),
        P("dp"),
        P("dp"),
        P("dp", None),
        P("dp"),
        P("dp"),
        P("dp", None),
        P("dp"),
        P("dp"),
        P("dp"),
        P("dp", None),
        P("dp"),
        P("dp", None),
        P("dp"),
    )
    return jax.shard_map(shards, mesh=mesh, in_specs=in_specs, out_specs=out_specs, check_vma=False)
```

profile of v0, /device:TPU:0, one launch (start us, length us, event | category | flops | bytes accessed | tf_op | source)
XLA Modules:
  0.0 793.2 jit_solution(6325828315978471569)
XLA Ops:
  7.2 0.7 all-gather.5.cloned.1.call-update
  8.0 0.7 all-gather.7.cloned.1.call-update
  8.7 0.7 all-gather.9.cloned.1.call-update
  10.0 0.8 dynamic-update-slice
  10.9 0.8 dynamic-update-slice.1
  11.7 0.8 dynamic-update-slice.2
  12.6 0.8 dynamic-update-slice.3
  13.4 0.8 dynamic-update-slice.4
  14.2 0.8 dynamic-update-slice.5
  15.1 0.8 dynamic-update-slice.6
  15.9 0.8 dynamic-update-slice.8
  16.7 0.8 dynamic-update-slice.7
  17.6 42.6 %all-reduce.19 = (bf16[768]{0:T(1024)(128)(2,1)S(1)}, bf16[768]{0:T(1024)(128)(2,1)S(1)}, bf16[768]{0:T(1024)(128)(2,1)S(1)}, bf16[768]{0:T(1024)(128)(2,1)S(1)}...) all-reduce(bf16[768]{0:T(1024)(128)(2,1)S(1)} %dynamic-update-slice, ...), channel_id=1, replica_groups=mesh['dp'=32] {'dp'}, use_global_device_ids=true, to_apply=%add.1 | all-reduce | flops 9216 | bytes 36864
  60.2 1.3 reshape.169
  62.3 1.0 reshape.198
  63.7 10.1 %all-gather.5.cloned.1.call-done = bf16[768,2304]{1,0:T(8,128)(2,1)} async-done(((bf16[24,2304]{1,0:T(8,128)(2,1)}), bf16[768,2304]{1,0:T(8,128)(2,1)}) %all-gather.5.cloned.1.call-update) | async-done | bytes 3538960 | tf_op jit(solution)/shard_map/all_gather | solution.py:47
  73.8 5.8 copy.51
  79.7 4.1 fusion.42
  83.7 0.9 multiply_reduce_fusion.1
  84.7 0.9 exponential_reduce_fusion
  85.8 1.5 copy-done
  87.4 1.1 convolution_convert_fusion.1
  88.5 41.3 %all-gather.7.cloned.1.call-done = bf16[768,768]{1,0:T(8,128)(2,1)} async-done(((bf16[24,768]{1,0:T(8,128)(2,1)}), bf16[768,768]{1,0:T(8,128)(2,1)}) %all-gather.7.cloned.1.call-update) | async-done | bytes 1179664 | tf_op jit(solution)/shard_map/all_gather | solution.py:50
  129.7 2.1 fusion.64
  131.8 1.1 copy-done.2
  133.2 62.1 %all-gather.9.cloned.1.call-done = bf16[768,3072]{1,0:T(8,128)(2,1)} async-done(((bf16[24,3072]{1,0:T(8,128)(2,1)}), bf16[768,3072]{1,0:T(8,128)(2,1)}) %all-gather.9.cloned.1.call-update) | async-done | bytes 4718608 | tf_op jit(solution)/shard_map/all_gather | solution.py:56
  195.2 6.4 fusion.38
  201.7 2.3 copy-done.9
  204.0 12.9 %multiply_convert_fusion.1 = (bf16[2,197,3072]{2,1,0:T(8,128)(2,1)}, f32[2,197,3072]{2,1,0:T(8,128)}) fusion(f32[2,197,3072]{2,1,0:T(8,128)S(1)} %get-tuple-element.56, f32[3072]{0:T(1024)S(1)} %convert_element_type.136, u8[197,3072]{1,0:T(8,128)(4,1)S(1)} %get-tuple-element.16, u8[197,3072]{1,0:T(8,128)(4,1)S(1)} %get-tuple-element.15), kind=kLoop, calls=%fused_computation.14 | loop fusion | flops 85936128 | bytes 13326336 | tf_op jit(solution)/shard_map/convert_element_type | solution.py:88
  216.8 43.7 %all-gather.11.cloned.1.call-done = bf16[3072,768]{1,0:T(8,128)(2,1)} async-done(((bf16[96,768]{1,0:T(8,128)(2,1)}), bf16[3072,768]{1,0:T(8,128)(2,1)}) %all-gather.11.cloned.1.call-update) | async-done | bytes 4718608 | tf_op jit(solution)/shard_map/all_gather | solution.py:58
  260.5 8.0 %convert_reduce_fusion = (f32[3072]{0:T(1024)S(1)}, bf16[2,197,3072]{2,1,0:T(8,128)(2,1)S(1)}) fusion(f32[2,197,3072]{2,1,0:T(8,128)} %get-tuple-element.47, bf16[3072,768]{1,0:T(8,128)(2,1)} %all-gather.11.cloned.1.call-done, f32[2,197,768]{2,1,0:T(8,128)S(1)} %reshape.172, f32[2,197]{1,0:T(2,128)S(1)} %mul.210, f32[2,197,3072]{2,1,0:T(8,128)} %copy-done.9, ...), kind=kOutput, calls=%fused_computation.10 | convolution fusion | flops 1880303616 | bytes 18058792 | tf_op jit(solution)/shard_map/gtd,fd->gtf/dot_general | solution.py:102
  268.6 5.7 multiply_reduce_fusion.2
  274.8 1.0 copy-done.5
  276.1 0.8 copy-done.11
  276.9 2.3 convolution_bitcast_fusion.3
  279.4 0.8 copy-done.8
  280.3 1.0 convert_element_type.125
  281.2 3.0 convolution_convert_fusion.2
  284.2 1.4 copy.54
  285.6 4.6 multiply_reduce_fusion
  290.3 1.1 multiply_convert_fusion
  291.6 0.9 fusion.36
  292.5 0.7 convert_reduce_fusion.2
  293.3 1.1 convert_reduce_fusion.1
  295.3 1.4 copy-done.14
  296.6 5.0 convolution_bitcast_fusion.2
  301.7 8.5 %convolution_bitcast_fusion.1 = f32[768,3072]{1,0:T(8,128)} fusion(bf16[2,197,3072]{2,1,0:T(8,128)(2,1)} %copy-done.18, f32[2,197,768]{2,1,0:T(8,128)} %copy-done.2, f32[768]{0:T(1024)S(1)} %convert_element_type.134, f32[768]{0:T(1024)S(1)} %convert_element_type.133, f32[2,197]{1,0:T(2,128)S(1)} %fusion.56, f32[2,197]{1,0:T(2,128)S(1)} %broadcast_multiply_fusion), kind=kOutput, calls=%fused_computation.2 | convolution fusion | flops 1860638208 | bytes 13077584 | tf_op jit(solution)/shard_map/gtd,gtf->df/dot_general | solution.py:105
  310.6 8.1 %convolution_bitcast_fusion = f32[3072,768]{1,0:T(8,128)} fusion(bf16[2,197,3072]{2,1,0:T(8,128)(2,1)} %get-tuple-element.46, f32[2,197,768]{2,1,0:T(8,128)S(1)} %reshape.172, f32[2,197]{1,0:T(2,128)S(1)} %mul.210), kind=kOutput, calls=%fused_computation.1 | convolution fusion | flops 1859730432 | bytes 13069864 | tf_op jit(solution)/shard_map/gtf,gtd->fd/dot_general | solution.py:101
  318.9 0.9 copy-done.13
  320.1 4.9 fusion.60
  325.0 1.0 copy-done.10
  326.6 40.7 %all-reduce.18 = (f32[768]{0:T(1024)S(1)}, f32[768]{0:T(1024)S(1)}, f32[768]{0:T(1024)S(1)}, f32[768]{0:T(1024)S(1)}, f32[768]{0:T(1024)S(1)}, /*index=5*/f32[76...) all-reduce(f32[768]{0:T(1024)S(1)} %get-tuple-element.17, ...), channel_id=2, replica_groups=mesh['dp'=32] {'dp'}, use_global_device_ids=true, to_apply=%region_12.0.clone | all-reduce | flops 9216 | bytes 73728
  367.4 0.6 dynamic-slice
  368.0 0.6 dynamic-slice.1
  368.5 0.6 dynamic-slice.2
  369.1 0.6 dynamic-slice.3
  372.0 3.2 add_add_fusion.2
  375.3 2.5 reshape.175
  377.8 5.2 fusion.33
  383.0 0.9 reshape.171
  383.9 0.6 dynamic-slice.7
  384.5 118.1 %reduce-scatter.5.cloned.1.call-done = f32[24,2304]{1,0:T(8,128)} async-done(((f32[768,2304]{1,0:T(8,128)}), f32[24,2304]{1,0:T(8,128)}) %reduce-scatter.5.cloned.1.call-update) | async-done | bytes 221200 | tf_op jit(solution)/shard_map/reduce_scatter | solution.py:161
  502.6 141.1 %reduce-scatter.9.cloned.1.call-done = f32[24,3072]{1,0:T(8,128)} async-done(((f32[768,3072]{1,0:T(8,128)}), f32[24,3072]{1,0:T(8,128)}) %reduce-scatter.9.cloned.1.call-update) | async-done | bytes 294928 | tf_op jit(solution)/shard_map/reduce_scatter | solution.py:161
  643.7 142.4 %reduce-scatter.11.cloned.1.call-done = f32[96,768]{1,0:T(8,128)} async-done(((f32[3072,768]{1,0:T(8,128)}), f32[96,768]{1,0:T(8,128)}) %reduce-scatter.11.cloned.1.call-update) | async-done | bytes 294928 | tf_op jit(solution)/shard_map/reduce_scatter | solution.py:161
  (101 shorter events, 8.3 us)
Async XLA Ops:
  7.2 54.3 %copy-start.6 = (bf16[394,768]{1,0:T(8,128)(2,1)S(1)}, bf16[394,768]{1,0:T(8,128)(2,1)}, u32[]{:S(2)}) copy-start(bf16[394,768]{1,0:T(8,128)(2,1)} %param.16) | copy-start | bytes 1815556
  7.2 66.7 %all-gather.5.cloned.1.call-start = ((), (), s32[]{:S(2)}) async-start(), calls=%async_computation.4 | async-start | bytes 3649536 | tf_op jit(solution)/shard_map/all_gather | solution.py:47
  7.9 121.8 %all-gather.7.cloned.1.call-start = ((), (), s32[]{:S(2)}) async-start(), calls=%async_computation.5 | async-start | bytes 1216512 | tf_op jit(solution)/shard_map/all_gather | solution.py:50
  8.7 186.6 %all-gather.9.cloned.1.call-start = ((), (), s32[]{:S(2)}) async-start(), calls=%async_computation.6 | async-start | bytes 4866048 | tf_op jit(solution)/shard_map/all_gather | solution.py:56
  9.4 251.1 %all-gather.11.cloned.1.call-start = ((), (), s32[]{:S(2)}) async-start(), calls=%async_computation.7 | async-start | bytes 4866048 | tf_op jit(solution)/shard_map/all_gather | solution.py:58
  10.0 374.5 %reduce-scatter.7.cloned.1.call-start = ((), (), s32[]{:S(2)}) async-start(), calls=%async_computation.9 | async-start | bytes 2433024 | tf_op jit(solution)/shard_map/reduce_scatter | solution.py:161
  60.2 3.3 copy-start.17
  60.2 3.4 copy-start.12
  62.3 1.2 copy-start.7
  73.8 5.8 copy-start.16
  83.7 2.1 copy-start.1
  84.7 2.7 copy-start
  131.8 1.1 copy-start.2
  201.7 2.3 copy-start.9
  260.5 8.1 %copy-start.3 = (f32[2,197,768]{2,1,0:T(8,128)S(1)}, f32[2,197,768]{2,1,0:T(8,128)}, u32[]{:S(2)}) copy-start(f32[2,197,768]{2,1,0:T(8,128)} %copy-done.2) | copy-start | bytes 3631108
  268.5 5.7 copy-start.18
  274.8 1.0 copy-start.5
  276.1 0.8 copy-start.11
  279.2 1.1 copy-start.8
  279.2 223.4 %reduce-scatter.5.cloned.1.call-start = ((), (), s32[]{:S(2)}) async-start(), calls=%async_computation.8 | async-start | bytes 7299072 | tf_op jit(solution)/shard_map/reduce_scatter | solution.py:161
  285.6 4.7 slice-start
  285.6 4.7 slice-start.1
  285.6 5.8 slice-start.2
  290.3 1.4 slice-start.3
  295.0 1.7 copy-start.15
  295.3 1.4 copy-start.14
  301.7 342.0 %reduce-scatter.9.cloned.1.call-start = ((), (), s32[]{:S(2)}) async-start(), calls=%async_computation.10 | async-start | bytes 9732096 | tf_op jit(solution)/shard_map/reduce_scatter | solution.py:161
  310.3 475.8 %reduce-scatter.11.cloned.1.call-start = ((), (), s32[]{:S(2)}) async-start(), calls=%async_computation.11 | async-start | bytes 9732096 | tf_op jit(solution)/shard_map/reduce_scatter | solution.py:161
  318.7 1.1 copy-start.13
  325.0 1.0 copy-start.10
  375.3 2.5 copy-start.4
Sparse Core Ops, SparseCore 0:
  10.9 62.8 all-gather.4
  76.7 52.9 all-gather.6
  132.6 62.5 all-gather.8
  198.0 62.4 all-gather.10
  279.3 97.9 reduce-scatter.6
  384.4 118.1 reduce-scatter.4
  509.1 134.6 reduce-scatter.8
  651.2 134.8 reduce-scatter.10
where the time goes:
time: 803 us; the launch traced here: 793 us
  waiting for transfers between devices  561 us (70%)
  blocking collectives  83.3 us (10%)
  matrix products  72.7 us (9%)
  local copies, waits for them, and re-layouts  38.9 us (5%)
  other arithmetic  21.4 us (3%)
  between operations  14.8 us (2%)
    reduce_scatter x4, waiting for transfers between devices, shards(): lax.psum_scatter(attn_grads + mlp_grads, 'dp', scatter_dimension=0, tiled...  402 us
    unnamed x2, blocking collectives  83.3 us
    all_gather x1, waiting for transfers between devices, shards(): lax.all_gather(up_weight, 'dp', axis=0, tiled=True)  62.1 us
    all_gather x1, waiting for transfers between devices, shards(): lax.all_gather(down_weight, 'dp', axis=0, tiled=True)  43.7 us
    all_gather x1, waiting for transfers between devices, shards(): lax.all_gather(out_weight, 'dp', axis=0, tiled=True)  41.3 us
    unnamed x73, local copies, waits for them, and re-layouts  24.1 us
  transfers between devices with their start and end apart: 8, of which 7 were waited for; matrix products, arithmetic and copies ran while one was open for 13% of the time, Pallas kernels for 0%

commit v1 on v0

--- a/solution.py
+++ b/solution.py
@@ -7,6 +7,18 @@
 HEADS = 12
 HEAD_DIM = 64
 LEN = 197
+
+
+def gather_by_bits(shard, axis, dim):
+    ways, here = (lax.axis_size(axis), lax.axis_index(axis))
+    grown, reach = (shard, 1)
+    while reach < ways:
+        theirs = lax.ppermute(grown, axis, [(d, d ^ reach) for d in range(ways)])
+        mine_first = jnp.concatenate([grown, theirs], axis=dim)
+        theirs_first = jnp.concatenate([theirs, grown], axis=dim)
+        grown = jnp.where(here & reach == 0, mine_first, theirs_first)
+        reach = 2 * reach
+    return grown
 
 
 def layer_norm(values, gain, shift):
@@ -53,7 +65,7 @@
     mlp_full = (
         lax.all_gather(gain_second, "dp", axis=0, tiled=True),
         lax.all_gather(shift_second, "dp", axis=0, tiled=True),
-        lax.all_gather(up_weight, "dp", axis=0, tiled=True),
+        gather_by_bits(up_weight, "dp", 0),
         lax.all_gather(up_bias, "dp", axis=0, tiled=True),
         lax.all_gather(down_weight, "dp", axis=0, tiled=True),
         lax.all_gather(down_bias, "dp", axis=0, tiled=True),

time: 803 us -> 876 us (1.091)
  waiting for transfers between devices: 561 us -> 605 us
  blocking collectives: 83.3 us -> 98.9 us
  matrix products: 72.7 us -> 86 us
    all_gather x1, waiting for transfers between devices: 41.3 us -> 94.3 us  [shards(): lax.all_gather(out_weight, 'dp', axis=0, tiled=True)]
    ppermute x0 -> x5, waiting for transfers between devices: none -> 22.4 us  [gather_by_bits(): theirs = lax.ppermute(grown, axis, [(d, d ^ reach) for d in range(ways)])]
    all_gather x1, waiting for transfers between devices: 62.1 us -> 45.2 us  [shards(): lax.all_gather(up_weight, 'dp', axis=0, tiled=True)]
    unnamed x2, blocking collectives: 83.3 us -> 98.9 us
    dot_general x1, matrix products: 8.04 us -> 20 us  [shards(): jnp.einsum('gtd,fd->gtf', d_mlp, back_down, preferred_element_type=f32)]
    all_gather x1, waiting for transfers between devices: 10.1 us -> 0.01 us  [shards(): lax.all_gather(packed_weight, 'dp', axis=0, tiled=True)]
    unnamed x73 -> x89, local copies, waits for them, and re-layouts: 24.1 us -> 17.9 us
  transfers between devices with their start and end apart: 8 -> 13, of which waited for: 7 -> 9; matrix products, arithmetic and copies ran while one was open for 13% -> 14% of each run, Pallas kernels for 0% -> 0%
where the time goes in v1:
time: 876 us; the launch traced here: 872 us
  waiting for transfers between devices  605 us (69%)
  blocking collectives  98.9 us (11%)
  matrix products  86 us (10%)
  local copies, waits for them, and re-layouts  31.5 us (4%)
  other arithmetic  27 us (3%)
  between operations  14.9 us (2%)
  starting transfers between devices  8.83 us (1%)
    reduce_scatter x4, waiting for transfers between devices, shards(): lax.psum_scatter(attn_grads + mlp_grads, 'dp', scatter_dimension=0, tiled...  401 us
    unnamed x2, blocking collectives  98.9 us
    all_gather x1, waiting for transfers between devices, shards(): lax.all_gather(out_weight, 'dp', axis=0, tiled=True)  94.3 us
    all_gather x1, waiting for transfers between devices, shards(): lax.all_gather(up_weight, 'dp', axis=0, tiled=True)  45.2 us
    all_gather x1, waiting for transfers between devices, shards(): lax.all_gather(down_weight, 'dp', axis=0, tiled=True)  39.7 us
    ppermute x5, waiting for transfers between devices, gather_by_bits(): theirs = lax.ppermute(grown, axis, [(d, d ^ reach) for d in range(ways)])  22.4 us
    dot_general x1, matrix products, shards(): jnp.einsum('gtd,fd->gtf', d_mlp, back_down, preferred_element_type=f32)  20 us
    unnamed x89, local copies, waits for them, and re-layouts  17.9 us
  transfers between devices with their start and end apart: 13, of which 9 were waited for; matrix products, arithmetic and copies ran while one was open for 14% of the time, Pallas kernels for 0%

profile of v1, /device:TPU:0, one launch (start us, length us, event | category | flops | bytes accessed | tf_op | source)
XLA Modules:
  0.0 872.2 jit_solution(3928317394045998907)
XLA Ops:
  7.3 0.7 all-gather.5.cloned.1.call-update
  8.1 0.7 all-gather.7.cloned.1.call-update
  8.8 0.7 all-gather.9.cloned.1.call-update
  10.1 1.2 collective-permute-done
  11.3 1.0 maximum_select_fusion.4
  12.3 2.9 collective-permute-start.1
  15.2 7.3 collective-permute-done.1
  22.7 1.8 collective-permute-start.2
  24.5 13.9 %collective-permute-done.2 = bf16[96,3072]{1,0:T(8,128)(2,1)S(1)} collective-permute-done((bf16[96,3072]{1,0:T(8,128)(2,1)S(1)}, bf16[96,3072]{1,0:T(8,128)(2,1)S(1)}, u32[]{:S(2)}, u32[]{:S(2)}) %collective-permute-start.2) | collective-permute-done | bytes 589856 | tf_op jit(solution)/shard_map/ppermute | solution.py:16
  38.4 1.3 maximum_select_fusion.2
  39.6 1.5 collective-permute-start.3
  43.4 58.2 %all-reduce.19 = (bf16[768]{0:T(1024)(128)(2,1)S(1)}, bf16[768]{0:T(1024)(128)(2,1)S(1)}, bf16[768]{0:T(1024)(128)(2,1)S(1)}, bf16[768]{0:T(1024)(128)(2,1)S(1)}...) all-reduce(bf16[768]{0:T(1024)(128)(2,1)S(1)} %dynamic-update-slice, ...), channel_id=1, replica_groups=mesh['dp'=32] {'dp'}, use_global_device_ids=true, to_apply=%add.1 | all-reduce | flops 9216 | bytes 36864
  102.6 1.0 reshape.198
  104.0 3.8 maximum_select_fusion.1
  107.8 1.6 collective-permute-start.4
  109.4 5.8 copy.51
  115.2 4.1 fusion.52
  119.3 0.9 multiply_reduce_fusion.1
  120.2 0.9 exponential_reduce_fusion
  121.4 1.5 copy-done
  122.9 1.1 convolution_convert_fusion.1
  124.0 94.3 %all-gather.7.cloned.1.call-done = bf16[768,768]{1,0:T(8,128)(2,1)} async-done(((bf16[24,768]{1,0:T(8,128)(2,1)}), bf16[768,768]{1,0:T(8,128)(2,1)}) %all-gather.7.cloned.1.call-update) | async-done | bytes 1179664 | tf_op jit(solution)/shard_map/all_gather | solution.py:62
  218.4 2.1 fusion.75
  220.7 7.6 fusion.48
  228.4 2.3 copy-done.9
  230.6 12.2 %multiply_convert_fusion.1 = (bf16[2,197,3072]{2,1,0:T(8,128)(2,1)}, f32[2,197,3072]{2,1,0:T(8,128)}) fusion(f32[2,197,3072]{2,1,0:T(8,128)S(1)} %get-tuple-element.56, u8[197,3072]{1,0:T(8,128)(4,1)S(1)} %get-tuple-element.16, u8[197,3072]{1,0:T(8,128)(4,1)S(1)} %get-tuple-element.15), kind=kLoop, calls=%fused_computation.14 | loop fusion | flops 84725760 | bytes 13314048 | tf_op jit(solution)/shard_map/convert_element_type | solution.py:100
  242.9 39.7 %all-gather.9.cloned.1.call-done = bf16[3072,768]{1,0:T(8,128)(2,1)} async-done(((bf16[96,768]{1,0:T(8,128)(2,1)}), bf16[3072,768]{1,0:T(8,128)(2,1)}) %all-gather.9.cloned.1.call-update) | async-done | bytes 4718608 | tf_op jit(solution)/shard_map/all_gather | solution.py:70
  282.5 20.0 %convert_reduce_fusion = (f32[3072]{0:T(1024)S(1)}, bf16[2,197,3072]{2,1,0:T(8,128)(2,1)}) fusion(f32[2,197,3072]{2,1,0:T(8,128)} %get-tuple-element.47, f32[2,197,3072]{2,1,0:T(8,128)} %copy-done.9, bf16[3072,768]{1,0:T(8,128)(2,1)} %all-gather.9.cloned.1.call-done, f32[2,197,768]{2,1,0:T(8,128)S(1)} %reshape.172, f32[2,197]{1,0:T(2,128)S(1)} %mul.210), kind=kOutput, calls=%fused_computation.10 | convolution fusion | flops 1879093248 | bytes 18046504 | tf_op jit(solution)/shard_map/gtd,fd->gtf/dot_general | solution.py:114
  302.5 45.2 %all-gather.11.cloned.1.call-done = bf16[768,3072]{1,0:T(8,128)(2,1)} async-done(((bf16[24,3072]{1,0:T(8,128)(2,1)}), bf16[768,3072]{1,0:T(8,128)(2,1)}) %all-gather.11.cloned.1.call-update) | async-done | bytes 4718608 | tf_op jit(solution)/shard_map/all_gather | solution.py:107
  347.8 5.9 multiply_reduce_fusion.2
  354.2 1.0 copy-done.5
  355.5 0.8 copy-done.11
  356.3 2.2 convolution_bitcast_fusion.3
  358.6 1.0 copy-done.8
  359.6 1.0 convert_element_type.125
  360.6 3.0 convolution_convert_fusion.2
  363.6 1.4 copy.54
  365.0 4.6 multiply_reduce_fusion
  369.6 1.1 multiply_convert_fusion
  371.0 0.9 fusion.46
  371.9 0.7 convert_reduce_fusion.2
  372.6 1.1 convert_reduce_fusion.1
  374.6 1.4 copy-done.14
  376.1 5.0 convolution_bitcast_fusion.2
  381.1 8.1 convolution_bitcast_fusion
  389.5 8.5 convolution_bitcast_fusion.1
  398.2 0.9 copy-done.13
  399.4 4.9 fusion.71
  404.4 1.1 copy-done.10
  406.0 40.7 %all-reduce.18 = (f32[768]{0:T(1024)S(1)}, f32[768]{0:T(1024)S(1)}, f32[768]{0:T(1024)S(1)}, f32[768]{0:T(1024)S(1)}, f32[768]{0:T(1024)S(1)}, /*index=5*/f32[76...) all-reduce(f32[768]{0:T(1024)S(1)} %get-tuple-element.17, ...), channel_id=2, replica_groups=mesh['dp'=32] {'dp'}, use_global_device_ids=true, to_apply=%region_12.13.clone | all-reduce | flops 9216 | bytes 73728
  446.7 0.6 dynamic-slice
  447.3 0.6 dynamic-slice.1
  447.9 0.6 dynamic-slice.2
  448.5 0.6 dynamic-slice.3
  449.1 0.6 dynamic-slice.4
  449.7 0.6 dynamic-slice.5
  451.4 3.3 add_add_fusion.2
  454.7 2.5 reshape.175
  457.3 5.2 fusion.43
  462.4 0.9 reshape.171
  463.4 0.6 dynamic-slice.7
  464.0 117.8 %reduce-scatter.5.cloned.1.call-done = f32[24,2304]{1,0:T(8,128)} async-done(((f32[768,2304]{1,0:T(8,128)}), f32[24,2304]{1,0:T(8,128)}) %reduce-scatter.5.cloned.1.call-update) | async-done | bytes 221200 | tf_op jit(solution)/shard_map/reduce_scatter | solution.py:173
  581.8 141.2 %reduce-scatter.11.cloned.1.call-done = f32[96,768]{1,0:T(8,128)} async-done(((f32[3072,768]{1,0:T(8,128)}), f32[96,768]{1,0:T(8,128)}) %reduce-scatter.11.cloned.1.call-update) | async-done | bytes 294928 | tf_op jit(solution)/shard_map/reduce_scatter | solution.py:173
  723.0 142.1 %reduce-scatter.9.cloned.1.call-done = f32[24,3072]{1,0:T(8,128)} async-done(((f32[768,3072]{1,0:T(8,128)}), f32[24,3072]{1,0:T(8,128)}) %reduce-scatter.9.cloned.1.call-update) | async-done | bytes 294928 | tf_op jit(solution)/shard_map/reduce_scatter | solution.py:173
  (131 shorter events, 9.3 us)
Async XLA Ops:
  7.2 34.0 %copy-start.18 = (bf16[24]{0:T(256)(128)(2,1)S(1)}, bf16[24]{0:T(256)(128)(2,1)}, u32[]{:S(2)}) copy-start(bf16[24]{0:T(256)(128)(2,1)} %param.18) | copy-start | bytes 148
  7.2 34.3 %copy-start.19 = (bf16[24]{0:T(256)(128)(2,1)S(1)}, bf16[24]{0:T(256)(128)(2,1)}, u32[]{:S(2)}) copy-start(bf16[24]{0:T(256)(128)(2,1)} %param.19) | copy-start | bytes 148
  7.2 34.5 %copy-start.20 = (bf16[24]{0:T(256)(128)(2,1)S(1)}, bf16[24]{0:T(256)(128)(2,1)}, u32[]{:S(2)}) copy-start(bf16[24]{0:T(256)(128)(2,1)} %param.22) | copy-start | bytes 148
  7.2 34.7 %copy-start.21 = (bf16[24]{0:T(256)(128)(2,1)S(1)}, bf16[24]{0:T(256)(128)(2,1)}, u32[]{:S(2)}) copy-start(bf16[24]{0:T(256)(128)(2,1)} %param.21) | copy-start | bytes 148
  7.2 35.0 %copy-start.22 = (bf16[24]{0:T(256)(128)(2,1)S(1)}, bf16[24]{0:T(256)(128)(2,1)}, u32[]{:S(2)}) copy-start(bf16[24]{0:T(256)(128)(2,1)} %param.24) | copy-start | bytes 148
  7.2 35.2 %copy-start.23 = (bf16[24]{0:T(256)(128)(2,1)S(1)}, bf16[24]{0:T(256)(128)(2,1)}, u32[]{:S(2)}) copy-start(bf16[24]{0:T(256)(128)(2,1)} %param.25) | copy-start | bytes 148
  7.2 35.4 %copy-start.24 = (bf16[24]{0:T(256)(128)(2,1)S(1)}, bf16[24]{0:T(256)(128)(2,1)}, u32[]{:S(2)}) copy-start(bf16[24]{0:T(256)(128)(2,1)} %param.26) | copy-start | bytes 148
  7.3 35.6 %copy-start.25 = (bf16[24]{0:T(256)(128)(2,1)S(1)}, bf16[24]{0:T(256)(128)(2,1)}, u32[]{:S(2)}) copy-start(bf16[24]{0:T(256)(128)(2,1)} %param.30) | copy-start | bytes 148
  7.3 35.9 %copy-start.26 = (bf16[96]{0:T(256)(128)(2,1)S(1)}, bf16[96]{0:T(256)(128)(2,1)}, u32[]{:S(2)}) copy-start(bf16[96]{0:T(256)(128)(2,1)} %param.28) | copy-start | bytes 580
  7.3 94.3 %copy-start.6 = (bf16[394,768]{1,0:T(8,128)(2,1)S(1)}, bf16[394,768]{1,0:T(8,128)(2,1)}, u32[]{:S(2)}) copy-start(bf16[394,768]{1,0:T(8,128)(2,1)} %param.16) | copy-start | bytes 1815556
  7.3 102.1 %all-gather.5.cloned.1.call-start = ((), (), s32[]{:S(2)}) async-start(), calls=%async_computation.4 | async-start | bytes 3649536 | tf_op jit(solution)/shard_map/all_gather | solution.py:59
  8.0 210.3 %all-gather.7.cloned.1.call-start = ((), (), s32[]{:S(2)}) async-start(), calls=%async_computation.5 | async-start | bytes 1216512 | tf_op jit(solution)/shard_map/all_gather | solution.py:62
  8.8 273.8 %all-gather.9.cloned.1.call-start = ((), (), s32[]{:S(2)}) async-start(), calls=%async_computation.6 | async-start | bytes 4866048 | tf_op jit(solution)/shard_map/all_gather | solution.py:70
  9.5 338.3 %all-gather.11.cloned.1.call-start = ((), (), s32[]{:S(2)}) async-start(), calls=%async_computation.7 | async-start | bytes 4866048 | tf_op jit(solution)/shard_map/all_gather | solution.py:107
  9.5 1.7 collective-permute-start
  12.3 10.2 %collective-permute-start.1 = (bf16[48,3072]{1,0:T(8,128)(2,1)S(1)}, bf16[48,3072]{1,0:T(8,128)(2,1)S(1)}, u32[]{:S(2)}, u32[]{:S(2)}) collective-permute-start(bf16[48,3072]{1,0:T(8,128)(2,1)S(1)} %maximum_select_fusion.4), channel_id=1, source_target_pairs={{0,2},{1,3},{2,0},{3,1},{4,6},{5,7},{6,4},{7,5},{8,10},{9,11},{10,... | collective-permute-start | bytes 884744 | tf_op jit(solution)/shard_map/ppermute | solution.py:16
  22.7 15.7 %collective-permute-start.2 = (bf16[96,3072]{1,0:T(8,128)(2,1)S(1)}, bf16[96,3072]{1,0:T(8,128)(2,1)S(1)}, u32[]{:S(2)}, u32[]{:S(2)}) collective-permute-start(bf16[96,3072]{1,0:T(8,128)(2,1)S(1)} %maximum_select_fusion.3), channel_id=1, source_target_pairs={{0,4},{1,5},{2,6},{3,7},{4,0},{5,1},{6,2},{7,3},{8,12},{9,13},{10,... | collective-permute-start | bytes 1769480 | tf_op jit(solution)/shard_map/ppermute | solution.py:16
  39.6 64.4 %collective-permute-start.3 = (bf16[192,3072]{1,0:T(8,128)(2,1)}, bf16[192,3072]{1,0:T(8,128)(2,1)}, u32[]{:S(2)}, u32[]{:S(2)}) collective-permute-start(bf16[192,3072]{1,0:T(8,128)(2,1)} %maximum_select_fusion.2), channel_id=1, source_target_pairs={{0,8},{1,9},{2,10},{3,11},{4,12},{5,13},{6,14},{7,15},{8,0},{9,1},... | collective-permute-start | bytes 3538952 | tf_op jit(solution)/shard_map/ppermute | solution.py:16
  41.1 422.8 %reduce-scatter.7.cloned.1.call-start = ((), (), s32[]{:S(2)}) async-start(), calls=%async_computation.9 | async-start | bytes 2433024 | tf_op jit(solution)/shard_map/reduce_scatter | solution.py:173
  101.6 2.2 copy-start.17
  101.6 2.3 copy-start.12
  102.6 1.2 copy-start.7
  107.8 112.9 %collective-permute-start.4 = (bf16[384,3072]{1,0:T(8,128)(2,1)}, bf16[384,3072]{1,0:T(8,128)(2,1)}, u32[]{:S(2)}, u32[]{:S(2)}) collective-permute-start(bf16[384,3072]{1,0:T(8,128)(2,1)} %maximum_select_fusion.1), channel_id=1, source_target_pairs={{0,16},{1,17},{2,18},{3,19},{4,20},{5,21},{6,22},{7,23},{8,24},{9,... | collective-permute-start | bytes 7077896 | tf_op jit(solution)/shard_map/ppermute | solution.py:16
  109.4 5.8 copy-start.15
  119.3 2.1 copy-start.1
  120.2 2.7 copy-start
  220.4 7.9 copy-start.2
  228.4 2.3 copy-start.9
  347.8 5.9 copy-start.3
  354.2 1.0 copy-start.5
  355.5 0.8 copy-start.11
  358.5 1.1 copy-start.8
  358.6 223.2 %reduce-scatter.5.cloned.1.call-start = ((), (), s32[]{:S(2)}) async-start(), calls=%async_computation.8 | async-start | bytes 7299072 | tf_op jit(solution)/shard_map/reduce_scatter | solution.py:173
  364.9 4.7 slice-start
  364.9 4.7 slice-start.1
  365.0 5.8 slice-start.2
  369.6 1.4 slice-start.3
  374.3 1.7 copy-start.16
  374.6 1.4 copy-start.14
  381.1 341.9 %reduce-scatter.11.cloned.1.call-start = ((), (), s32[]{:S(2)}) async-start(), calls=%async_computation.11 | async-start | bytes 9732096 | tf_op jit(solution)/shard_map/reduce_scatter | solution.py:173
  389.3 475.9 %reduce-scatter.9.cloned.1.call-start = ((), (), s32[]{:S(2)}) async-start(), calls=%async_computation.10 | async-start | bytes 9732096 | tf_op jit(solution)/shard_map/reduce_scatter | solution.py:173
  398.0 1.1 copy-start.13
  404.4 1.1 copy-start.10
  454.7 2.5 copy-start.4
Sparse Core Ops, SparseCore 0:
  11.0 67.6 all-gather.4
  81.6 136.7 all-gather.6
  221.3 61.2 all-gather.8
  285.3 62.4 all-gather.10
  358.7 97.7 reduce-scatter.6
  463.5 118.2 reduce-scatter.4
  588.3 134.6 reduce-scatter.10
  730.5 134.6 reduce-scatter.8
